TPU v7x, 32 devices: a whole 2x2x4 slice. The times are simulated.
32 devices in a mesh: slide: 4 (over x, core), seq: 8 (over z, y).
Axes of the slice: x: 2, y: 2, z: 4, core: 2. Of those that a mesh axis runs over, the one named last changes fastest.
Arguments:
- tiles: bfloat16 [32768, 768], P(('slide', 'seq')), may hold values from -6 to 6
- route: int32 [32768], P(('slide', 'seq')), may hold values from 0 to 32767, as said below
- counts: int32 [4], replicated, may hold values from 2048 to 8192, as said below
- w_qkv: bfloat16 [768, 2304], replicated
- w_out: bfloat16 [768, 768], replicated, may hold values from -0.21875 to 0.21875
Outputs:
- mixed: bfloat16 [32768, 768], P(('slide', 'seq'))
Inputs may be any that keep to these rules, and one draw needn't show every extreme that they name: `route`: every position of the 4 x 8192 sequences is named exactly once. The rows of one loader device (aligned blocks of 1024 rows) name either 16 or 48 positions in each aligned block of 1024 positions, and exactly 48 in some of them. `counts`: at least one slide is full.
All inputs are finite; a program needn't handle non-finite values.
Results may differ from a plain program's by a relative error of at most 0.0067.
Values may be sent and summed in bfloat16 or wider, within the bound.
A program may use at most 128 MiB of HBM per device.

v0:
```python
import functools
import math

import jax
import jax.numpy as jnp
from jax import lax
from jax.experimental import pallas as pl
from jax.experimental.pallas import tpu as pltpu
from jax.sharding import PartitionSpec as P

HEADS = 16
RATE_MID = 4
PAIRS = HEADS // 2
LANES = 128
NT = (((1,), (1,)), ((), ()))
BF = jnp.bfloat16
F32 = jnp.float32


def iota(shape, dim):
    return lax.broadcasted_iota(jnp.int32, shape, dim)


def dot(a, b):
    return jnp.dot(a, b, preferred_element_type=F32)


def dot_nt(a, b):
    return lax.dot_general(a, b, NT, preferred_element_type=F32)


def position_of(row, rows, n_seq):
    half = rows // 2
    run = half // n_seq
    seg = row // half
    block = (row % half) // run
    index = row % run
    group = n_seq // RATE_MID
    residue = (block % group) * RATE_MID + block // group
    return seg * half + index * n_seq + residue


def row_of(position, rows, n_seq):
    half = rows // 2
    run = half // n_seq
    seg = position // half
    within = position % half
    residue = within % n_seq
    block = (residue % RATE_MID) * (n_seq // RATE_MID) + residue // RATE_MID
    return seg * half + block * run + within // n_seq


def block_of(residue, n_seq):
    return (residue % RATE_MID) * (n_seq // RATE_MID) + residue // RATE_MID


def layer_norm(values):
    mean = jnp.mean(values, -1, keepdims=True)
    centred = values - mean
    var = jnp.mean(centred * centred, -1, keepdims=True)
    return centred * lax.rsqrt(var + 1e-05)


def dispatch_kernel(owners, most, n_seq, route_ref, tiles_ref, out_ref):
    rows = tiles_ref.shape[0]
    slots = owners * most
    target = route_ref[...] // rows
    mine = iota((owners, rows), 0) == target
    upper = (iota((rows, rows), 0) <= iota((rows, rows), 1)).astype(BF)
    counted = dot(mine.astype(BF), upper)
    rank = jnp.sum(jnp.where(mine, counted, 0.0), 0, keepdims=True).astype(jnp.int32) - 1
    slot = target * most + rank
    move = (iota((slots, rows), 0) == slot).astype(BF)
    width = tiles_ref.shape[1]
    out_ref[:, :width] = dot(move, tiles_ref[...]).astype(BF)
    local = row_of(route_ref[...] % rows, rows, n_seq)
    kind = iota((LANES, rows), 0)
    digits = jnp.where(
        kind == 0, local // 32, jnp.where(kind == 1, local % 32, jnp.where(kind == 2, 1, 0))
    )
    out_ref[:, width:] = dot_nt(move, digits.astype(F32).astype(BF)).astype(BF)


def project_kernel(n_seq, limit_ref, arrived_ref, w_ref, placed_ref, q_ref, k_ref,
                   v_ref, mid_ref, wide_ref):
    rows = placed_ref.shape[0]
    half = rows // 2
    run = half // n_seq
    step = half // RATE_MID
    slots = arrived_ref.shape[0]
    features = placed_ref.shape[1]
    unit = (iota((8, LANES), 0) == iota((8, LANES), 1)).astype(BF)
    sent = dot_nt(unit, arrived_ref[:, features:])
    place = sent[0:1] * 32.0 + sent[1:2] + (1.0 - sent[2:3]) * (2.0 * rows)
    take = (iota((rows, slots), 0) == place.astype(jnp.int32)).astype(BF)
    placed = dot(take, arrived_ref[:, :features])
    placed_ref[...] = placed.astype(BF)
    normed = layer_norm(placed).astype(BF)
    lane = iota((rows, 2 * LANES), 1) % LANES
    position = position_of(iota((rows, 2 * LANES), 0), rows, n_seq)
    valid = position < limit_ref[0]
    flag = (lane == 96) | (lane == 97)
    ones = jnp.where(flag, 1.0, 0.0)
    bias = jnp.where(flag & jnp.logical_not(valid), -1e30, 0.0)
    width = PAIRS * LANES
    for couple in range(0, PAIRS, 2):
        for part, (ref, extra) in enumerate(((q_ref, ones), (k_ref, bias), (v_ref, ones))):
            start = part * width + couple * LANES
            both = (dot(normed, w_ref[:, start : start + 2 * LANES]) + extra).astype(BF)
            for pair in (couple, couple + 1):
                value = both[:, (pair - couple) * LANES : (pair - couple + 1) * LANES]
                ref[pair] = value
                for seg in range(2):
                    owner = pair % RATE_MID
                    base = seg * half + owner * step
                    mid_ref[owner, pair // RATE_MID, part, seg * step : (seg + 1) * step] = (
                        value[base : base + step]
                    )
                    for residue in range(pair, n_seq, PAIRS):
                        base = seg * half + block_of(residue, n_seq) * run
                        wide_ref[residue, part, seg * run : (seg + 1) * run] = value[
                            base : base + run
                        ]


def one_head(query, keys, values, head, factor):
    lane = iota(query.shape, 1)
    own = ((lane >= 48 * head) & (lane < 48 * head + 48)) | (lane == 96 + head)
    query = jnp.where(own, query, jnp.zeros_like(query))
    scores = dot_nt(query, keys)
    top = jnp.max(scores, -1, keepdims=True)
    weights = jnp.exp2((scores - top) * factor).astype(BF)
    result = dot(weights, values)
    total = result[:, 96:97]
    return result * (1.0 / total), top * factor + jnp.log2(total)


def near_kernel(factor, q_ref, k_ref, v_ref, out_ref):
    rows = q_ref.shape[1]
    half = rows // 2
    block = 256
    for seg in range(2):
        keys = k_ref[0, seg * half : (seg + 1) * half]
        values = v_ref[0, seg * half : (seg + 1) * half]
        for start in range(seg * half, (seg + 1) * half, block):
            query = q_ref[0, start : start + block]
            result_a, log_a = one_head(query, keys, values, 0, factor)
            result_b, log_b = one_head(query, keys, values, 1, factor)
            lane = iota(result_a.shape, 1)
            packed = jnp.where(lane < 48, result_a, result_b)
            packed = jnp.where(lane == 96, log_a, packed)
            packed = jnp.where(lane == 97, log_b, packed)
            out_ref[0, start : start + block] = packed


def pieces(value):
    first = value.astype(BF).astype(F32)
    second = (value - first).astype(BF).astype(F32)
    return first, second, value - first - second


def far_kernel(factor, ref, out_ref):
    count, taken = ref.shape[0], ref.shape[3]
    total = count * taken
    keys = ref[:, 0, 1].reshape(total, LANES)
    values = ref[:, 0, 2].reshape(total, LANES)
    for source in range(count):
        query = ref[source, 0, 0]
        result_a, log_a = one_head(query, keys, values, 0, factor)
        result_b, log_b = one_head(query, keys, values, 1, factor)
        lane = iota(result_a.shape, 1)
        packed = jnp.where(lane < 48, result_a, result_b)
        for index, piece in enumerate(pieces(log_a) + pieces(log_b)):
            packed = jnp.where(lane == 96 + index, piece, packed)
        out_ref[source, 0] = packed.astype(BF)


def merge_kernel(n_seq, limit_ref, first_ref, second_ref, third_ref, mid_ref, wide_ref, w_ref,
                 placed_ref, out_ref, att_ref):
    rows = placed_ref.shape[0]
    half = rows // 2
    run = half // n_seq
    step = half // RATE_MID
    group = n_seq // RATE_MID

    def log_of(packed, head):
        at = 96 + 3 * head
        return packed[:, at : at + 1] + packed[:, at + 1 : at + 2] + packed[:, at + 2 : at + 3]

    for pair in range(PAIRS):
        if pair < 3:
            near_ref = first_ref.at[pair]
        elif pair < 6:
            near_ref = second_ref.at[pair - 3]
        else:
            near_ref = third_ref.at[pair - 6]
        near_all = near_ref[...]
        lane = iota(near_all.shape, 1)
        att_ref[pair] = jnp.where(lane < 96, near_all, 0.0).astype(BF)
        mid_all = mid_ref[pair % RATE_MID, pair // RATE_MID].astype(F32)
        lane = iota((run, LANES), 1)
        for seg in range(2):
            base = seg * half + (pair % RATE_MID) * step
            for index in range(group):
                part = slice(base + index * run, base + (index + 1) * run)
                near = near_ref[part]
                at = seg * step + index * run
                mid = mid_all[at : at + run]
                merged = []
                for head in range(2):
                    residue = (pair + head * PAIRS) % n_seq
                    log_near, log_mid = near[:, 96 + head : 97 + head], log_of(mid, head)
                    top = jnp.maximum(log_near, log_mid)
                    has_wide = residue // RATE_MID == index
                    if has_wide:
                        wide = wide_ref[residue, seg * run : (seg + 1) * run].astype(F32)
                        log_wide = log_of(wide, head)
                        top = jnp.maximum(top, log_wide)
                    weight_near, weight_mid = jnp.exp2(log_near - top), jnp.exp2(log_mid - top)
                    numer = near * weight_near + mid * weight_mid
                    denom = weight_near + weight_mid
                    if has_wide:
                        weight_wide = jnp.exp2(log_wide - top)
                        numer += wide * weight_wide
                        denom += weight_wide
                    merged.append(numer * (1.0 / denom))
                both = jnp.where(lane < 48, merged[0], jnp.where(lane < 96, merged[1], 0.0))
                att_ref[pair, part] = both.astype(BF)

    limit = limit_ref[0]
    unsort = (row_of(iota((half, half), 0), rows, n_seq) == iota((half, half), 1)).astype(BF)
    for seg in range(2):
        part = slice(seg * half, (seg + 1) * half)
        attended = jnp.concatenate([att_ref[pair, part] for pair in range(PAIRS)], 1)
        projected = dot(attended, w_ref[...])
        mixed = placed_ref[part].astype(F32) + layer_norm(projected)
        position = iota(mixed.shape, 0) + seg * half
        mixed = dot(unsort, mixed.astype(BF))
        out_ref[part] = jnp.where(position < limit, mixed, 0.0).astype(BF)


def body(tiles, route, counts, w_qkv, w_out):
    rows, width = tiles.shape
    n_slide = lax.axis_size("slide")
    n_seq = lax.axis_size("seq")
    owners = n_slide * n_seq
    most = 3 * rows // (2 * owners)
    slots = owners * most
    head_dim = width // HEADS
    factor = math.log2(math.e) / math.sqrt(head_dim)
    padded = PAIRS * LANES
    vmem = pl.BlockSpec(memory_space=pltpu.VMEM)
    smem = pl.BlockSpec(memory_space=pltpu.SMEM)
    big = pltpu.CompilerParams(vmem_limit_bytes=48 << 20)

    seq_index = lax.axis_index("seq")
    slide_index = lax.axis_index("slide")
    both_axes = ("slide", "seq")
    outgoing = pl.pallas_call(
        functools.partial(dispatch_kernel, owners, most, n_seq),
        out_shape=jax.ShapeDtypeStruct((slots, width + LANES), BF),
        in_specs=[vmem, vmem],
        out_specs=vmem,
        compiler_params=big,
        name="dispatch",
    )(route.reshape(1, rows), tiles)
    exchange = functools.partial(lax.all_to_all, split_axis=0, concat_axis=0, tiled=True)
    sent_width = width + LANES
    arrived = exchange(outgoing.reshape(owners, most, sent_width), both_axes)
    arrived = arrived.reshape(slots, sent_width)

    column = jnp.arange(padded)
    lane = column % LANES
    source = (column // LANES + PAIRS * (lane // head_dim)) * head_dim + lane % head_dim
    source = jnp.where(lane < 2 * head_dim, source, -1)
    pick = (jnp.arange(width)[:, None] == source[None, :]).astype(BF)
    w_in = jnp.concatenate(
        [dot(w_qkv[:, i * width : (i + 1) * width], pick).astype(BF) for i in range(3)], 1
    )
    w_back = lax.dot_general(
        pick, w_out, (((0,), (0,)), ((), ())), preferred_element_type=F32
    ).astype(BF)

    limit = (counts[slide_index] - seq_index * rows).reshape(1)
    heads_shape = jax.ShapeDtypeStruct((PAIRS, rows, LANES), BF)
    mid_taken, wide_taken = rows // RATE_MID, rows // n_seq
    mid_pairs = PAIRS // RATE_MID
    placed, query, keys, values, mid_local, wide_local = pl.pallas_call(
        functools.partial(project_kernel, n_seq),
        out_shape=(
            jax.ShapeDtypeStruct((rows, width), BF),
            heads_shape,
            heads_shape,
            heads_shape,
            jax.ShapeDtypeStruct((RATE_MID, mid_pairs, 3, mid_taken, LANES), BF),
            jax.ShapeDtypeStruct((n_seq, 3, wide_taken, LANES), BF),
        ),
        in_specs=[smem, vmem, vmem],
        out_specs=(vmem,) * 6,
        compiler_params=big,
        name="project",
    )(limit, arrived, w_in)

    groups = [[start + i for i in range(RATE_MID)] for start in range(0, n_seq, RATE_MID)]
    wide_qkv = exchange(wide_local, "seq")
    def near(first, count):
        spec = pl.BlockSpec((1, rows, LANES), lambda i: (i + first, 0, 0))
        return pl.pallas_call(
            functools.partial(near_kernel, factor),
            out_shape=jax.ShapeDtypeStruct((count, rows, LANES), F32),
            grid=(count,),
            in_specs=[spec] * 3,
            out_specs=pl.BlockSpec((1, rows, LANES), lambda i: (i, 0, 0)),
            compiler_params=big,
            cost_estimate=pl.CostEstimate(
                flops=4 * count * rows * rows * LANES,
                bytes_accessed=10 * rows * LANES * count,
                transcendentals=count * rows * rows,
            ),
            name="near",
        )(query, keys, values)

    near_first, near_second, near_third = near(0, 3), near(3, 3), near(6, 2)

    def far(array):
        count, pairs, _, taken, _ = array.shape
        return pl.pallas_call(
            functools.partial(far_kernel, factor),
            out_shape=jax.ShapeDtypeStruct((count, pairs, taken, LANES), BF),
            grid=(pairs,),
            in_specs=[pl.BlockSpec((count, 1, 3, taken, LANES), lambda i: (0, i, 0, 0, 0))],
            out_specs=pl.BlockSpec((count, 1, taken, LANES), lambda i: (0, i, 0, 0)),
            compiler_params=big,
            cost_estimate=pl.CostEstimate(
                flops=8 * pairs * (count * taken) ** 2 * LANES,
                bytes_accessed=8 * pairs * count * taken * LANES,
                transcendentals=2 * pairs * (count * taken) ** 2,
            ),
            name="far",
        )(array)

    wide_qkv, mid_local, near_first = lax.optimization_barrier((wide_qkv, mid_local, near_first))
    mid_qkv = exchange(mid_local, "seq", axis_index_groups=groups)
    wide_out = far(wide_qkv.reshape(n_seq, 1, 3, wide_taken, LANES))
    wide_out, near_second = lax.optimization_barrier((wide_out, near_second))
    wide_back = exchange(wide_out.reshape(n_seq, wide_taken, LANES), "seq")
    mid_out = far(mid_qkv)
    mid_back = exchange(mid_out, "seq", axis_index_groups=groups)

    return pl.pallas_call(
        functools.partial(merge_kernel, n_seq),
        out_shape=jax.ShapeDtypeStruct((rows, width), BF),
        in_specs=[smem] + [vmem] * 7,
        out_specs=vmem,
        scratch_shapes=[pltpu.VMEM((PAIRS, rows, LANES), BF)],
        compiler_params=big,
        name="merge",
    )(limit, near_first, near_second, near_third, mid_back, wide_back, w_back, placed)


def solution(mesh):
    return jax.shard_map(
        body,
        mesh=mesh,
        in_specs=(P(("slide", "seq"), None), P(("slide", "seq")), P(), P(), P()),
        out_specs=P(("slide", "seq"), None),
        check_vma=False,
    )
```

profile of v0, /device:TPU:0, one launch (start us, length us, event | category | flops | bytes accessed | tf_op | source)
XLA Modules:
  0.0 193.2 jit_solution(12893347432227867186)
XLA Ops:
  0.0 0.0 copy-start
  0.0 1.5 copy-done.11
  1.5 0.7 copy-done.17
  2.2 3.8 %dispatch.1 = bf16[1536,896]{1,0:T(8,128)(2,1)S(1)} custom-call(s32[1,1024]{1,0:T(1,128)S(1)} %bitcast.16, bf16[1024,768]{1,0:T(8,128)(2,1)S(1)} %copy-done.11), custom_call_target="tpu_custom_call" | custom-call | tf_op jit(solution)/shard_map/dispatch/pallas_call | solution.py:259
  6.0 0.0 copy-start.4
  6.0 1.6 copy-done.4
  7.6 7.6 %all-to-all-start = ((bf16[32,48,896]{2,1,0:T(8,128)(2,1)}), bf16[32,48,896]{2,1,0:T(8,128)(2,1)}, u32[]{:S(2)}, u32[]{:S(2)}) async-start(bf16[32,48,896]{2,1,0:T(8,128)(2,1)} %bitcast.14), calls=%async_computation | async-start | bytes 5505024 | tf_op jit(solution)/shard_map/all_to_all | solution.py:269
  15.2 0.0 copy-done.19
  15.2 0.6 dynamic_slice.3
  16.5 0.0 copy-start.18
  16.5 2.9 %fusion.12 = bf16[768,1024]{1,0:T(8,128)(2,1)S(1)} fusion(s32[1024]{0:T(1024)S(1)} %fusion.27, bf16[768,2304]{1,0:T(8,128)(2,1)} %param.8), kind=kOutput, calls=%fused_computation.14 | convolution fusion | flops 1209532416 | bytes 2756608 | tf_op jit(solution)/shard_map/dot_general | solution.py:25
  19.4 0.0 copy-done.18
  19.4 1.4 fusion.13
  20.8 1.5 fusion.14
  22.3 2.3 %pad_maximum_fusion.w_ref = bf16[768,3072]{1,0:T(8,128)(2,1)} fusion(bf16[768,1024]{1,0:T(8,128)(2,1)S(1)} %fusion.12, bf16[768,1024]{1,0:T(8,128)(2,1)S(1)} %fusion.13, bf16[768,1024]{1,0:T(8,128)(2,1)S(1)} %fusion.14), kind=kLoop, calls=%fused_computation | loop fusion | flops 14155776 | bytes 9437184 | tf_op jit(solution)/shard_map/concatenate | solution.py:277
  24.6 55.0 %all-to-all-done = bf16[32,48,896]{2,1,0:T(8,128)(2,1)} async-done(((bf16[32,48,896]{2,1,0:T(8,128)(2,1)}), bf16[32,48,896]{2,1,0:T(8,128)(2,1)}, u32[]{:S(2)}, u32[]{:S(2)}) %all-to-all-start) | async-done | bytes 2752544 | tf_op jit(solution)/shard_map/all_to_all | solution.py:269
  79.6 14.1 %project.1 = (bf16[1024,768]{1,0:T(8,128)(2,1)S(1)}, bf16[8,1024,128]{2,1,0:T(8,128)(2,1)S(1)}, bf16[8,1024,128]{2,1,0:T(8,128)(2,1)}, bf16[8,1024,128]{2,1,0:T(...) custom-call(s32[1]{0:T(128)} %bitcast.1.limit_ref, ...), custom_call_target="tpu_custom_call" | custom-call | tf_op jit(solution)/shard_map/project/pallas_call | solution.py:288
  93.7 1.2 copy-done.12
  94.9 1.2 copy-done.13
  96.0 0.9 copy-done.14
  96.9 4.6 %all-to-all-start.1 = ((bf16[8,3,128,128]{3,2,1,0:T(8,128)(2,1)}), bf16[8,3,128,128]{3,2,1,0:T(8,128)(2,1)}, u32[]{:S(2)}, u32[]{:S(2)}) async-start(bf16[8,3,128,128]{3,2,1,0:T(8,128)(2,1)} %copy-done.14), calls=%async_computation.1 | async-start | bytes 1572864 | tf_op jit(solution)/shard_map/all_to_all | solution.py:305
  101.6 0.0 copy-start.1
  101.6 1.6 copy-done.1
  103.2 9.1 %near.3.first_ref = f32[3,1024,128]{2,1,0:T(8,128)S(1)} custom-call(bf16[8,1024,128]{2,1,0:T(8,128)(2,1)S(1)} %get-tuple-element.18.q_ref, bf16[8,1024,128]{2,1,0:T(8,128)(2,1)S(1)} %copy-done.1, bf16[8,1024,128]{2,1,0:T(8,128)(2,1)} %get-tuple-element.20.v_ref), custom_call_target="tpu_custom_call" | custom-call | flops 1610612736 | bytes 3932160 | tf_op jit(solution)/shard_map/near/pallas_call | solution.py:308
  112.3 0.0 copy-start.5
  112.3 1.1 copy-done.5
  113.4 8.5 %all-to-all-done.1 = bf16[8,3,128,128]{3,2,1,0:T(8,128)(2,1)} async-done(((bf16[8,3,128,128]{3,2,1,0:T(8,128)(2,1)}), bf16[8,3,128,128]{3,2,1,0:T(8,128)(2,1)}, u32[]{:S(2)}, u32[]{:S(2)}) %all-to-all-start.1) | async-done | bytes 786464 | tf_op jit(solution)/shard_map/all_to_all | solution.py:305
  121.9 4.3 %all-to-all-start.2 = ((bf16[4,2,3,256,128]{4,3,2,1,0:T(8,128)(2,1)}), bf16[4,2,3,256,128]{4,3,2,1,0:T(8,128)(2,1)}, u32[]{:S(2)}, u32[]{:S(2)}) async-start(bf16[4,2,3,256,128]{4,3,2,1,0:T(8,128)(2,1)} %copy-done.13), calls=%async_computation.2 | async-start | bytes 3145728 | tf_op jit(solution)/shard_map/all_to_all | solution.py:343
  126.3 0.0 copy-start.2
  126.3 1.6 copy-done.2
  127.9 9.1 %near.4.second_ref = f32[3,1024,128]{2,1,0:T(8,128)S(1)} custom-call(bf16[8,1024,128]{2,1,0:T(8,128)(2,1)S(1)} %get-tuple-element.18.q_ref, bf16[8,1024,128]{2,1,0:T(8,128)(2,1)S(1)} %copy-done.2, bf16[8,1024,128]{2,1,0:T(8,128)(2,1)} %get-tuple-element.20.v_ref), custom_call_target="tpu_custom_call" | custom-call | flops 1610612736 | bytes 3932160 | tf_op jit(solution)/shard_map/near/pallas_call | solution.py:308
  137.0 1.1 copy-done.7
  138.1 6.9 %far.2 = bf16[8,1,128,128]{3,2,1,0:T(8,128)(2,1)S(1)} custom-call(bf16[8,1,3,128,128]{4,3,2,1,0:T(8,128)(2,1)} %bitcast.8.ref), custom_call_target="tpu_custom_call" | custom-call | flops 1073741824 | bytes 1048576 | tf_op jit(solution)/shard_map/far/pallas_call | solution.py:327
  145.0 0.7 copy-done.16
  145.8 0.0 all-to-all-done.2.ref
  145.8 4.2 %all-to-all-start.4 = ((bf16[8,128,128]{2,1,0:T(8,128)(2,1)}), bf16[8,128,128]{2,1,0:T(8,128)(2,1)S(1)}, u32[]{:S(2)}, u32[]{:S(2)}) async-start(bf16[8,128,128]{2,1,0:T(8,128)(2,1)} %bitcast.15), calls=%async_computation.4 | async-start | bytes 524288 | tf_op jit(solution)/shard_map/all_to_all | solution.py:346
  149.9 9.4 %far.3 = bf16[4,2,256,128]{3,2,1,0:T(8,128)(2,1)S(1)} custom-call(bf16[4,2,3,256,128]{4,3,2,1,0:T(8,128)(2,1)} %all-to-all-done.2.ref), custom_call_target="tpu_custom_call" | custom-call | flops 2147483648 | bytes 2097152 | tf_op jit(solution)/shard_map/far/pallas_call | solution.py:327
  159.3 0.8 copy-done.15
  160.1 0.0 all-to-all-done.4.wide_ref
  160.1 4.4 %all-to-all-start.3 = ((bf16[4,2,256,128]{3,2,1,0:T(8,128)(2,1)}), bf16[4,2,256,128]{3,2,1,0:T(8,128)(2,1)}, u32[]{:S(2)}, u32[]{:S(2)}) async-start(bf16[4,2,256,128]{3,2,1,0:T(8,128)(2,1)} %copy-done.15), calls=%async_computation.3 | async-start | bytes 1048576 | tf_op jit(solution)/shard_map/all_to_all | solution.py:348
  164.5 2.8 %fusion.7.w_ref = bf16[1024,768]{1,0:T(8,128)(2,1)} fusion(bf16[768,768]{1,0:T(8,128)(2,1)S(1)} %copy-done, s32[1024]{0:T(1024)S(1)} %fusion.27), kind=kOutput, calls=%fused_computation.9 | convolution fusion | flops 1209532416 | bytes 2756608 | tf_op jit(solution)/shard_map/dot_general | solution.py:280
  167.3 6.4 %near.5.third_ref = f32[2,1024,128]{2,1,0:T(8,128)S(1)} custom-call(bf16[8,1024,128]{2,1,0:T(8,128)(2,1)S(1)} %get-tuple-element.18.q_ref, bf16[8,1024,128]{2,1,0:T(8,128)(2,1)S(1)} %copy-done.3, bf16[8,1024,128]{2,1,0:T(8,128)(2,1)} %get-tuple-element.20.v_ref), custom_call_target="tpu_custom_call" | custom-call | flops 1073741824 | bytes 2621440 | tf_op jit(solution)/shard_map/near/pallas_call | solution.py:308
  173.7 1.0 copy-done.9
  174.7 0.0 all-to-all-done.3.mid_ref
  174.7 1.4 copy-done.6
  176.1 1.4 copy-done.8
  177.5 1.2 copy-done.10
  178.7 14.2 %merge.1 = bf16[1024,768]{1,0:T(8,128)(2,1)} custom-call(s32[1]{0:T(128)} %bitcast.1.limit_ref, f32[3,1024,128]{2,1,0:T(8,128)S(1)} %copy-done.6, f32[3,1024,128]{2,1,0:T(8,128)S(1)} %copy-done.8, f32[2,1024,128]{2,1,0:T(8,128)S(1)} %copy-done.10, bf16[4,2,256,128]{3,2,1,0:T(8,128)(2,1)} %all-to-all-done.3.mid_ref, ...), custom_call_target="tpu_custom_call" | custom-call | tf_op jit(solution)/shard_map/merge/pallas_call | solution.py:350
  (17 shorter events, 0.0 us)
Async XLA Ops:
  0.0 164.5 %copy-start = (bf16[768,768]{1,0:T(8,128)(2,1)S(1)}, bf16[768,768]{1,0:T(8,128)(2,1)}, u32[]{:S(2)}) copy-start(bf16[768,768]{1,0:T(8,128)(2,1)} %param.9) | copy-start | bytes 3538948
  0.0 1.5 copy-start.11
  1.5 0.7 copy-start.17
  6.0 1.6 copy-start.4
  7.6 7.6 %copy-start.19 = (s32[4]{0:T(128)S(1)}, s32[4]{0:T(128)}, u32[]{:S(2)}) copy-start(s32[4]{0:T(128)} %param.7) | copy-start | bytes 52
  7.6 72.0 %all-to-all-start = ((bf16[32,48,896]{2,1,0:T(8,128)(2,1)}), bf16[32,48,896]{2,1,0:T(8,128)(2,1)}, u32[]{:S(2)}, u32[]{:S(2)}) async-start(bf16[32,48,896]{2,1,0:T(8,128)(2,1)} %bitcast.14), calls=%async_computation | async-start | bytes 5505024 | tf_op jit(solution)/shard_map/all_to_all | solution.py:269
  16.5 2.9 %copy-start.18 = (bf16[768,2304]{1,0:T(8,128)(2,1)S(1)}, bf16[768,2304]{1,0:T(8,128)(2,1)}, u32[]{:S(2)}) copy-start(bf16[768,2304]{1,0:T(8,128)(2,1)} %param.8) | copy-start | bytes 10616836
  93.7 1.2 copy-start.12
  94.9 1.2 copy-start.13
  96.0 0.9 copy-start.14
  96.9 25.0 %all-to-all-start.1 = ((bf16[8,3,128,128]{3,2,1,0:T(8,128)(2,1)}), bf16[8,3,128,128]{3,2,1,0:T(8,128)(2,1)}, u32[]{:S(2)}, u32[]{:S(2)}) async-start(bf16[8,3,128,128]{3,2,1,0:T(8,128)(2,1)} %copy-done.14), calls=%async_computation.1 | async-start | bytes 1572864 | tf_op jit(solution)/shard_map/all_to_all | solution.py:305
  101.6 1.6 copy-start.1
  112.3 1.1 copy-start.5
  121.9 23.8 %all-to-all-start.2 = ((bf16[4,2,3,256,128]{4,3,2,1,0:T(8,128)(2,1)}), bf16[4,2,3,256,128]{4,3,2,1,0:T(8,128)(2,1)}, u32[]{:S(2)}, u32[]{:S(2)}) async-start(bf16[4,2,3,256,128]{4,3,2,1,0:T(8,128)(2,1)} %copy-done.13), calls=%async_computation.2 | async-start | bytes 3145728 | tf_op jit(solution)/shard_map/all_to_all | solution.py:343
  126.3 1.6 copy-start.2
  137.0 1.1 copy-start.7
  145.0 0.7 copy-start.16
  145.8 14.3 %all-to-all-start.4 = ((bf16[8,128,128]{2,1,0:T(8,128)(2,1)}), bf16[8,128,128]{2,1,0:T(8,128)(2,1)S(1)}, u32[]{:S(2)}, u32[]{:S(2)}) async-start(bf16[8,128,128]{2,1,0:T(8,128)(2,1)} %bitcast.15), calls=%async_computation.4 | async-start | bytes 524288 | tf_op jit(solution)/shard_map/all_to_all | solution.py:346
  159.3 0.8 copy-start.15
  160.1 14.6 %all-to-all-start.3 = ((bf16[4,2,256,128]{3,2,1,0:T(8,128)(2,1)}), bf16[4,2,256,128]{3,2,1,0:T(8,128)(2,1)}, u32[]{:S(2)}, u32[]{:S(2)}) async-start(bf16[4,2,256,128]{3,2,1,0:T(8,128)(2,1)} %copy-done.15), calls=%async_computation.3 | async-start | bytes 1048576 | tf_op jit(solution)/shard_map/all_to_all | solution.py:348
  164.5 2.8 %copy-start.3 = (bf16[8,1024,128]{2,1,0:T(8,128)(2,1)S(1)}, bf16[8,1024,128]{2,1,0:T(8,128)(2,1)}, u32[]{:S(2)}) copy-start(bf16[8,1024,128]{2,1,0:T(8,128)(2,1)} %get-tuple-element.19.k_ref) | copy-start | bytes 6291460
  173.7 1.0 copy-start.9
  174.7 1.4 copy-start.6
  176.1 1.4 copy-start.8
  177.5 1.2 copy-start.10
where the time goes:
time: 197 us; the launch traced here: 193 us
  Pallas kernels  73 us (37%)
  waiting for transfers between devices  63.5 us (32%)
  starting transfers between devices  25.1 us (13%)
  local copies, waits for them, and re-layouts  19.6 us (10%)
  matrix products  8.59 us (4%)
  other arithmetic  2.35 us (1%)
    all_to_all x1, waiting for transfers between devices, body(): arrived = exchange(outgoing.reshape(owners, most, sent_width), both_axes)  55 us
    pallas_call x3, Pallas kernels, near(): pl.pallas_call(functools.partial(near_kernel, factor), out_shape=jax.Shap...  24.6 us
    unnamed x40, local copies, waits for them, and re-layouts  19.1 us
    pallas_call x2, Pallas kernels, far(): pl.pallas_call(functools.partial(far_kernel, factor), out_shape=jax.Shape...  16.3 us
    pallas_call x1, Pallas kernels, body(): pl.pallas_call(functools.partial(merge_kernel, n_seq), out_shape=jax.Shap...  14.2 us
    pallas_call x1, Pallas kernels, body(): pl.pallas_call(functools.partial(project_kernel, n_seq), out_shape=(jax.S...  14.1 us
    all_to_all x1, waiting for transfers between devices, body(): wide_qkv = exchange(wide_local, 'seq')  8.5 us
    all_to_all x1, starting transfers between devices, body(): arrived = exchange(outgoing.reshape(owners, most, sent_width), both_axes)  7.59 us
  transfers between devices with their start and end apart: 5, of which 2 were waited for; matrix products, arithmetic and copies ran while one was open for 6% of the time, Pallas kernels for 21%

commit v1 on v0

--- a/solution.py
+++ b/solution.py
@@ -188,10 +188,10 @@
         return packed[:, at : at + 1] + packed[:, at + 1 : at + 2] + packed[:, at + 2 : at + 3]
 
     for pair in range(PAIRS):
-        if pair < 3:
+        if pair < 4:
             near_ref = first_ref.at[pair]
         elif pair < 6:
-            near_ref = second_ref.at[pair - 3]
+            near_ref = second_ref.at[pair - 4]
         else:
             near_ref = third_ref.at[pair - 6]
         near_all = near_ref[...]
@@ -320,7 +320,7 @@
             name="near",
         )(query, keys, values)
 
-    near_first, near_second, near_third = near(0, 3), near(3, 3), near(6, 2)
+    near_first, near_second, near_third = near(0, 4), near(4, 2), near(6, 2)
 
     def far(array):
         count, pairs, _, taken, _ = array.shape

time: 197 us -> 196 us (level)
  transfers between devices with their start and end apart: 5 -> 5, of which waited for: 2 -> 3; matrix products, arithmetic and copies ran while one was open for 6% -> 6% of each run, Pallas kernels for 21% -> 21%
where the time goes in v1:
time: 196 us; the launch traced here: 192 us
  Pallas kernels  72.7 us (37%)
  waiting for transfers between devices  63.9 us (33%)
  starting transfers between devices  24.6 us (13%)
  local copies, waits for them, and re-layouts  19.2 us (10%)
  matrix products  8.56 us (4%)
  other arithmetic  2.35 us (1%)
    all_to_all x1, waiting for transfers between devices, body(): arrived = exchange(outgoing.reshape(owners, most, sent_width), both_axes)  55 us
    pallas_call x3, Pallas kernels, near(): pl.pallas_call(functools.partial(near_kernel, factor), out_shape=jax.Shap...  24.6 us
    unnamed x40, local copies, waits for them, and re-layouts  18.6 us
    pallas_call x2, Pallas kernels, far(): pl.pallas_call(functools.partial(far_kernel, factor), out_shape=jax.Shape...  16.3 us
    pallas_call x1, Pallas kernels, body(): pl.pallas_call(functools.partial(project_kernel, n_seq), out_shape=(jax.S...  14.1 us
    pallas_call x1, Pallas kernels, body(): pl.pallas_call(functools.partial(merge_kernel, n_seq), out_shape=jax.Shap...  13.9 us
    all_to_all x1, starting transfers between devices, body(): arrived = exchange(outgoing.reshape(owners, most, sent_width), both_axes)  7.59 us
    all_to_all x1, waiting for transfers between devices, body(): wide_qkv = exchange(wide_local, 'seq')  7.13 us
  transfers between devices with their start and end apart: 5, of which 3 were waited for; matrix products, arithmetic and copies ran while one was open for 6% of the time, Pallas kernels for 21%

profile of v1, /device:TPU:0, one launch (start us, length us, event | category | flops | bytes accessed | tf_op | source)
XLA Modules:
  0.0 192.4 jit_solution(2204767514012662634)
XLA Ops:
  0.0 0.0 copy-start
  0.0 1.5 copy-done.9
  1.5 0.7 copy-done.17
  2.2 3.8 %dispatch.1 = bf16[1536,896]{1,0:T(8,128)(2,1)S(1)} custom-call(s32[1,1024]{1,0:T(1,128)S(1)} %bitcast.16, bf16[1024,768]{1,0:T(8,128)(2,1)S(1)} %copy-done.9), custom_call_target="tpu_custom_call" | custom-call | tf_op jit(solution)/shard_map/dispatch/pallas_call | solution.py:259
  6.0 0.0 copy-start.3
  6.0 1.6 copy-done.3
  7.6 7.6 %all-to-all-start = ((bf16[32,48,896]{2,1,0:T(8,128)(2,1)}), bf16[32,48,896]{2,1,0:T(8,128)(2,1)}, u32[]{:S(2)}, u32[]{:S(2)}) async-start(bf16[32,48,896]{2,1,0:T(8,128)(2,1)} %bitcast.14), calls=%async_computation | async-start | bytes 5505024 | tf_op jit(solution)/shard_map/all_to_all | solution.py:269
  15.2 0.0 copy-done.19
  15.2 0.6 dynamic_slice.3
  16.5 0.0 copy-start.18
  16.5 2.9 %fusion.12 = bf16[768,1024]{1,0:T(8,128)(2,1)S(1)} fusion(s32[1024]{0:T(1024)S(1)} %fusion.27, bf16[768,2304]{1,0:T(8,128)(2,1)} %param.8), kind=kOutput, calls=%fused_computation.14 | convolution fusion | flops 1209532416 | bytes 2756608 | tf_op jit(solution)/shard_map/dot_general | solution.py:25
  19.4 0.0 copy-done.18
  19.4 1.4 fusion.13
  20.8 1.5 fusion.14
  22.3 2.3 %pad_maximum_fusion.w_ref = bf16[768,3072]{1,0:T(8,128)(2,1)} fusion(bf16[768,1024]{1,0:T(8,128)(2,1)S(1)} %fusion.12, bf16[768,1024]{1,0:T(8,128)(2,1)S(1)} %fusion.13, bf16[768,1024]{1,0:T(8,128)(2,1)S(1)} %fusion.14), kind=kLoop, calls=%fused_computation | loop fusion | flops 14155776 | bytes 9437184 | tf_op jit(solution)/shard_map/concatenate | solution.py:277
  24.6 55.0 %all-to-all-done = bf16[32,48,896]{2,1,0:T(8,128)(2,1)} async-done(((bf16[32,48,896]{2,1,0:T(8,128)(2,1)}), bf16[32,48,896]{2,1,0:T(8,128)(2,1)}, u32[]{:S(2)}, u32[]{:S(2)}) %all-to-all-start) | async-done | bytes 2752544 | tf_op jit(solution)/shard_map/all_to_all | solution.py:269
  79.6 14.1 %project.1 = (bf16[1024,768]{1,0:T(8,128)(2,1)S(1)}, bf16[8,1024,128]{2,1,0:T(8,128)(2,1)S(1)}, bf16[8,1024,128]{2,1,0:T(8,128)(2,1)}, bf16[8,1024,128]{2,1,0:T(...) custom-call(s32[1]{0:T(128)} %bitcast.1.limit_ref, ...), custom_call_target="tpu_custom_call" | custom-call | tf_op jit(solution)/shard_map/project/pallas_call | solution.py:288
  93.7 1.1 copy-done.10
  94.8 1.1 copy-done.13
  96.0 0.9 copy-done.14
  96.8 4.6 %all-to-all-start.1 = ((bf16[8,3,128,128]{3,2,1,0:T(8,128)(2,1)}), bf16[8,3,128,128]{3,2,1,0:T(8,128)(2,1)}, u32[]{:S(2)}, u32[]{:S(2)}) async-start(bf16[8,3,128,128]{3,2,1,0:T(8,128)(2,1)} %copy-done.14), calls=%async_computation.1 | async-start | bytes 1572864 | tf_op jit(solution)/shard_map/all_to_all | solution.py:305
  101.5 11.9 %near.3.first_ref = f32[4,1024,128]{2,1,0:T(8,128)S(1)} custom-call(bf16[8,1024,128]{2,1,0:T(8,128)(2,1)S(1)} %get-tuple-element.18.q_ref, bf16[8,1024,128]{2,1,0:T(8,128)(2,1)} %get-tuple-element.19.k_ref, bf16[8,1024,128]{2,1,0:T(8,128)(2,1)} %get-tuple-element.20.v_ref), custom_call_target="tpu_custom_call" | custom-call | flops 2147483648 | bytes 5242880 | tf_op jit(solution)/shard_map/near/pallas_call | solution.py:308
  113.3 0.0 copy-start.4
  113.3 1.3 copy-done.4
  114.7 7.1 %all-to-all-done.1 = bf16[8,3,128,128]{3,2,1,0:T(8,128)(2,1)} async-done(((bf16[8,3,128,128]{3,2,1,0:T(8,128)(2,1)}), bf16[8,3,128,128]{3,2,1,0:T(8,128)(2,1)}, u32[]{:S(2)}, u32[]{:S(2)}) %all-to-all-start.1) | async-done | bytes 786464 | tf_op jit(solution)/shard_map/all_to_all | solution.py:305
  121.8 4.4 %all-to-all-start.2 = ((bf16[4,2,3,256,128]{4,3,2,1,0:T(8,128)(2,1)}), bf16[4,2,3,256,128]{4,3,2,1,0:T(8,128)(2,1)}, u32[]{:S(2)}, u32[]{:S(2)}) async-start(bf16[4,2,3,256,128]{4,3,2,1,0:T(8,128)(2,1)} %copy-done.13), calls=%async_computation.2 | async-start | bytes 3145728 | tf_op jit(solution)/shard_map/all_to_all | solution.py:343
  126.2 0.0 copy-start.1
  126.2 1.6 copy-done.1
  127.8 6.4 %near.4.second_ref = f32[2,1024,128]{2,1,0:T(8,128)S(1)} custom-call(bf16[8,1024,128]{2,1,0:T(8,128)(2,1)S(1)} %get-tuple-element.18.q_ref, bf16[8,1024,128]{2,1,0:T(8,128)(2,1)S(1)} %copy-done.1, bf16[8,1024,128]{2,1,0:T(8,128)(2,1)} %get-tuple-element.20.v_ref), custom_call_target="tpu_custom_call" | custom-call | flops 1073741824 | bytes 2621440 | tf_op jit(solution)/shard_map/near/pallas_call | solution.py:308
  134.2 0.0 copy-start.5
  134.2 1.0 copy-done.5
  135.1 7.0 %far.2 = bf16[8,1,128,128]{3,2,1,0:T(8,128)(2,1)S(1)} custom-call(bf16[8,1,3,128,128]{4,3,2,1,0:T(8,128)(2,1)} %bitcast.8.ref), custom_call_target="tpu_custom_call" | custom-call | flops 1073741824 | bytes 1048576 | tf_op jit(solution)/shard_map/far/pallas_call | solution.py:327
  142.1 0.7 copy-done.16
  142.8 1.8 all-to-all-done.2.ref
  144.6 3.7 %all-to-all-start.4 = ((bf16[8,128,128]{2,1,0:T(8,128)(2,1)}), bf16[8,128,128]{2,1,0:T(8,128)(2,1)S(1)}, u32[]{:S(2)}, u32[]{:S(2)}) async-start(bf16[8,128,128]{2,1,0:T(8,128)(2,1)} %bitcast.15), calls=%async_computation.4 | async-start | bytes 524288 | tf_op jit(solution)/shard_map/all_to_all | solution.py:346
  148.3 9.4 %far.3 = bf16[4,2,256,128]{3,2,1,0:T(8,128)(2,1)S(1)} custom-call(bf16[4,2,3,256,128]{4,3,2,1,0:T(8,128)(2,1)} %all-to-all-done.2.ref), custom_call_target="tpu_custom_call" | custom-call | flops 2147483648 | bytes 2097152 | tf_op jit(solution)/shard_map/far/pallas_call | solution.py:327
  157.7 0.8 copy-done.15
  158.5 0.0 all-to-all-done.4.wide_ref
  158.5 4.4 %all-to-all-start.3 = ((bf16[4,2,256,128]{3,2,1,0:T(8,128)(2,1)}), bf16[4,2,256,128]{3,2,1,0:T(8,128)(2,1)}, u32[]{:S(2)}, u32[]{:S(2)}) async-start(bf16[4,2,256,128]{3,2,1,0:T(8,128)(2,1)} %copy-done.15), calls=%async_computation.3 | async-start | bytes 1048576 | tf_op jit(solution)/shard_map/all_to_all | solution.py:348
  162.9 2.8 %fusion.7.w_ref = bf16[1024,768]{1,0:T(8,128)(2,1)} fusion(bf16[768,768]{1,0:T(8,128)(2,1)S(1)} %copy-done, s32[1024]{0:T(1024)S(1)} %fusion.27), kind=kOutput, calls=%fused_computation.9 | convolution fusion | flops 1209532416 | bytes 2756608 | tf_op jit(solution)/shard_map/dot_general | solution.py:280
  165.7 6.4 %near.5.third_ref = f32[2,1024,128]{2,1,0:T(8,128)S(1)} custom-call(bf16[8,1024,128]{2,1,0:T(8,128)(2,1)S(1)} %get-tuple-element.18.q_ref, bf16[8,1024,128]{2,1,0:T(8,128)(2,1)S(1)} %copy-done.2, bf16[8,1024,128]{2,1,0:T(8,128)(2,1)} %get-tuple-element.20.v_ref), custom_call_target="tpu_custom_call" | custom-call | flops 1073741824 | bytes 2621440 | tf_op jit(solution)/shard_map/near/pallas_call | solution.py:308
  172.1 1.0 copy-done.7
  173.1 0.0 all-to-all-done.3.mid_ref
  173.1 1.2 copy-done.6
  174.3 1.2 copy-done.8
  175.5 1.4 copy-done.11
  176.9 1.4 copy-done.12
  178.3 13.9 %merge.1 = bf16[1024,768]{1,0:T(8,128)(2,1)} custom-call(s32[1]{0:T(128)} %bitcast.1.limit_ref, f32[4,1024,128]{2,1,0:T(8,128)} %copy-done.4, f32[2,1024,128]{2,1,0:T(8,128)S(1)} %copy-done.6, f32[2,1024,128]{2,1,0:T(8,128)S(1)} %copy-done.8, bf16[4,2,256,128]{3,2,1,0:T(8,128)(2,1)} %all-to-all-done.3.mid_ref, ...), custom_call_target="tpu_custom_call" | custom-call | tf_op jit(solution)/shard_map/merge/pallas_call | solution.py:350
  (17 shorter events, 0.0 us)
Async XLA Ops:
  0.0 162.9 %copy-start = (bf16[768,768]{1,0:T(8,128)(2,1)S(1)}, bf16[768,768]{1,0:T(8,128)(2,1)}, u32[]{:S(2)}) copy-start(bf16[768,768]{1,0:T(8,128)(2,1)} %param.9) | copy-start | bytes 3538948
  0.0 1.5 copy-start.9
  1.5 0.7 copy-start.17
  6.0 1.6 copy-start.3
  7.6 7.6 %copy-start.19 = (s32[4]{0:T(128)S(1)}, s32[4]{0:T(128)}, u32[]{:S(2)}) copy-start(s32[4]{0:T(128)} %param.7) | copy-start | bytes 52
  7.6 72.0 %all-to-all-start = ((bf16[32,48,896]{2,1,0:T(8,128)(2,1)}), bf16[32,48,896]{2,1,0:T(8,128)(2,1)}, u32[]{:S(2)}, u32[]{:S(2)}) async-start(bf16[32,48,896]{2,1,0:T(8,128)(2,1)} %bitcast.14), calls=%async_computation | async-start | bytes 5505024 | tf_op jit(solution)/shard_map/all_to_all | solution.py:269
  16.5 2.9 %copy-start.18 = (bf16[768,2304]{1,0:T(8,128)(2,1)S(1)}, bf16[768,2304]{1,0:T(8,128)(2,1)}, u32[]{:S(2)}) copy-start(bf16[768,2304]{1,0:T(8,128)(2,1)} %param.8) | copy-start | bytes 10616836
  93.7 1.1 copy-start.10
  94.8 1.1 copy-start.13
  95.9 0.9 copy-start.14
  96.8 25.0 %all-to-all-start.1 = ((bf16[8,3,128,128]{3,2,1,0:T(8,128)(2,1)}), bf16[8,3,128,128]{3,2,1,0:T(8,128)(2,1)}, u32[]{:S(2)}, u32[]{:S(2)}) async-start(bf16[8,3,128,128]{3,2,1,0:T(8,128)(2,1)} %copy-done.14), calls=%async_computation.1 | async-start | bytes 1572864 | tf_op jit(solution)/shard_map/all_to_all | solution.py:305
  113.3 1.4 copy-start.4
  121.8 22.8 %all-to-all-start.2 = ((bf16[4,2,3,256,128]{4,3,2,1,0:T(8,128)(2,1)}), bf16[4,2,3,256,128]{4,3,2,1,0:T(8,128)(2,1)}, u32[]{:S(2)}, u32[]{:S(2)}) async-start(bf16[4,2,3,256,128]{4,3,2,1,0:T(8,128)(2,1)} %copy-done.13), calls=%async_computation.2 | async-start | bytes 3145728 | tf_op jit(solution)/shard_map/all_to_all | solution.py:343
  126.2 1.6 copy-start.1
  134.2 1.0 copy-start.5
  142.1 0.7 copy-start.16
  144.6 13.9 %all-to-all-start.4 = ((bf16[8,128,128]{2,1,0:T(8,128)(2,1)}), bf16[8,128,128]{2,1,0:T(8,128)(2,1)S(1)}, u32[]{:S(2)}, u32[]{:S(2)}) async-start(bf16[8,128,128]{2,1,0:T(8,128)(2,1)} %bitcast.15), calls=%async_computation.4 | async-start | bytes 524288 | tf_op jit(solution)/shard_map/all_to_all | solution.py:346
  157.7 0.8 copy-start.15
  158.5 14.6 %all-to-all-start.3 = ((bf16[4,2,256,128]{3,2,1,0:T(8,128)(2,1)}), bf16[4,2,256,128]{3,2,1,0:T(8,128)(2,1)}, u32[]{:S(2)}, u32[]{:S(2)}) async-start(bf16[4,2,256,128]{3,2,1,0:T(8,128)(2,1)} %copy-done.15), calls=%async_computation.3 | async-start | bytes 1048576 | tf_op jit(solution)/shard_map/all_to_all | solution.py:348
  162.9 2.8 %copy-start.2 = (bf16[8,1024,128]{2,1,0:T(8,128)(2,1)S(1)}, bf16[8,1024,128]{2,1,0:T(8,128)(2,1)}, u32[]{:S(2)}) copy-start(bf16[8,1024,128]{2,1,0:T(8,128)(2,1)} %get-tuple-element.19.k_ref) | copy-start | bytes 6291460
  172.1 1.0 copy-start.7
  173.1 1.2 copy-start.6
  174.3 1.2 copy-start.8
  175.5 1.4 copy-start.11
  176.9 1.4 copy-start.12
